TPU v7x, 32 devices: a whole 2x2x4 slice. The times are simulated.
32 devices in a mesh: gx: 2 (over x), gy: 4 (over y, core), gz: 4 (over z).
Axes of the slice: x: 2, y: 2, z: 4, core: 2. Of those that a mesh axis runs over, the one named last changes fastest.
Arguments:
- states: float32 [19, 32, 64, 512], P(None, 'gx', 'gy', 'gz'), may hold values from 0 to 1
- active: int32 [4, 4, 4], P('gx', 'gy', 'gz'), may hold values 0 or 1
- fibre_index: int32 [4, 4, 4], P('gx', 'gy', 'gz'), may hold values from 0 to 63
- fibre_angle: float32 [2, 64], replicated, may hold values from -3.140625 to 3.140625
- conduct: float32 [2, 64], replicated, may hold values from 0.05 to 0.3
- gate_half: float32 [17], replicated, may hold values from 0.1 to 0.9
- gate_slope: float32 [17], replicated, may hold values from 0.05 to 0.3
- gate_tau: float32 [17], replicated, may hold values from 2 to 60
- conductance: float32 [17], replicated, may hold values from 0.005 to 0.05
- reversal: float32 [17], replicated, may hold values from -1 to 1.5
- block_elem: int32 [16, 32, 16], P('gx', 'gy', 'gz'), may hold values from 0 to 8191, as said below
- block_weight: float32 [16, 32, 16], P('gx', 'gy', 'gz'), may hold values from 0.5 to 1.5
- node_disp: float32 [3, 16384], P(None, ('gx', 'gy', 'gz')), may hold values from -0.15 to 0.15
- elem_node: int32 [8, 8192], P(None, ('gx', 'gy', 'gz')), may hold values from 0 to 404, as said below
- elem_fibre: int32 [8192], P(('gx', 'gy', 'gz')), may hold values from 0 to 63
- material: float32 [3], replicated, may hold values from 0.5 to 2
Outputs:
- new_states: float32 [19, 32, 64, 512], P(None, 'gx', 'gy', 'gz')
- fine_disp: float32 [3, 32, 64, 512], P(None, 'gx', 'gy', 'gz')
- node_residual: float32 [3, 16384], P(None, ('gx', 'gy', 'gz'))
Inputs may be any that keep to these rules, and one draw needn't show every extreme that they name: `block_elem`: element numbers of the coarse partition: owner device e // 256, local element e % 256. Every element holds exactly one coupling block. Of the coupling blocks of one device at most 16 lie in elements of one owner device, and for every device some owner receives exactly 16 of them. `elem_node`: each column names eight distinct owner-local nodes of a hexahedral element of a structured partition, corner 4 i + 2 j + k at offset (i, j, k); neighbouring elements of one owner share nodes.
All inputs are finite; a program needn't handle non-finite values. No bound on the sum of `active` on one device may be relied on, other than what follows from the above.
Results may differ from a plain program's by a relative error of at most 0.0003.
Values sent between devices are 32-bit elements; how exact they have to be, the bound alone decides.
A program may use at most 64 MiB of HBM per device.

v0:
```python
import jax
import jax.numpy as jnp
from jax import lax
from jax.sharding import PartitionSpec as P

NSTATE = 19
TLX = 8
TLY = 16
TLZ = 128
SBX = 2
SBY = 2
SBZ = 32
FINE_STEPS = 2


calcium_keep = 0.9
tension_half = 0.09
highest = lax.Precision.HIGHEST


def padded_2(cells, sides, width):
    for axis, dim in sides:
        count = lax.axis_size(axis)
        ends = count - 1
        head = lax.slice_in_dim(cells, 0, width, axis=dim)
        tail = lax.slice_in_dim(cells, cells.shape[dim] - width, cells.shape[dim], axis=dim)
        cells = jnp.concatenate(
            [
                lax.ppermute(tail, axis, [(i, (i + 1) % count) for i in range(ends)]),
                cells,
                lax.ppermute(head, axis, [((i + 1) % count, i) for i in range(ends)]),
            ],
            axis=dim,
        )
    return cells


def fibre_frame(first_angle, second_angle):
    return jnp.stack(
        [
            jnp.cos(first_angle) * jnp.cos(second_angle),
            jnp.sin(first_angle) * jnp.cos(second_angle),
            jnp.sin(second_angle),
        ],
        0,
    )


def coefficients(frame, along, across, live_tile):
    spread = along - across
    return (
        jnp.stack(
            [
                across + spread * frame[0] * frame[0],
                across + spread * frame[1] * frame[1],
                across + spread * frame[2] * frame[2],
                spread * frame[0] * frame[1],
                spread * frame[0] * frame[2],
                spread * frame[1] * frame[2],
            ],
            0,
        )
        * live_tile
    )


def tile_lookup(fibre_index, fibre_angle, conduct):
    table = jnp.concatenate([fibre_frame(fibre_angle[0], fibre_angle[1]), conduct], 0)
    labels = jnp.arange(table.shape[1], dtype=jnp.int32)
    onehot = (fibre_index[None] == labels.reshape(-1, 1, 1, 1)).astype(jnp.float32)
    return jnp.sum(table.reshape(5, -1, 1, 1, 1) * onehot[None], axis=1)


def expand(tiles):
    return jnp.repeat(jnp.repeat(jnp.repeat(tiles, TLX, 1), TLY, 2), TLZ, 3)


def ionic(states, live, gate_half, gate_slope, gate_tau, conductance, reversal):
    volt = states[0]
    shape = (gate_half.shape[0],) + (1,) * (states.ndim - 1)
    steady = jax.nn.sigmoid((volt[None] - gate_half.reshape(shape)) / gate_slope.reshape(shape))
    keeping = jnp.exp(-1.0 / gate_tau).reshape(shape)
    old_gates = states[1 : NSTATE - 1]
    gates = steady + (old_gates - steady) * keeping
    current = jnp.sum(
        conductance.reshape(shape) * gates * (volt[None] - reversal.reshape(shape)), axis=0
    )
    vstar = volt - current
    calcium = states[NSTATE - 1] * calcium_keep + (1.0 - calcium_keep) * jax.nn.sigmoid(
        8.0 * (volt - 0.5)
    )
    alive = live > 0.5
    gates = jnp.where(alive[None], gates, old_gates)
    vstar = jnp.where(alive, vstar, volt)
    calcium = jnp.where(alive, calcium, states[NSTATE - 1])
    return (gates, vstar, calcium)


def fluxes(padded, coef):
    grad_x = (padded[2:, 1:-1, 1:-1] - padded[:-2, 1:-1, 1:-1]) * 0.5
    grad_y = (padded[1:-1, 2:, 1:-1] - padded[1:-1, :-2, 1:-1]) * 0.5
    grad_z = (padded[1:-1, 1:-1, 2:] - padded[1:-1, 1:-1, :-2]) * 0.5
    return jnp.stack(
        [
            coef[0] * grad_x + coef[3] * grad_y + coef[4] * grad_z,
            coef[3] * grad_x + coef[1] * grad_y + coef[5] * grad_z,
            coef[4] * grad_x + coef[5] * grad_y + coef[2] * grad_z,
        ],
        0,
    )


def divergence(flux):
    return (
        (flux[0, 2:, 1:-1, 1:-1] - flux[0, :-2, 1:-1, 1:-1]) * 0.5
        + (flux[1, 1:-1, 2:, 1:-1] - flux[1, 1:-1, :-2, 1:-1]) * 0.5
        + (flux[2, 1:-1, 1:-1, 2:] - flux[2, 1:-1, 1:-1, :-2]) * 0.5
    )


def corner_bits():
    corner = jnp.arange(8, dtype=jnp.int32)
    return jnp.stack([corner // 4, corner // 2 % 2, corner % 2], 1).astype(jnp.float32)


def shape_gradients():
    return (2.0 * corner_bits() - 1.0) * 0.25


def blend_weights():
    bits = corner_bits()
    place = jnp.arange(SBX * SBY * SBZ, dtype=jnp.int32)
    along_x = ((place // (SBY * SBZ)).astype(jnp.float32) + 0.5) / SBX
    along_y = ((place // SBZ % SBY).astype(jnp.float32) + 0.5) / SBY
    along_z = ((place % SBZ).astype(jnp.float32) + 0.5) / SBZ
    local = jnp.stack([along_x, along_y, along_z], 0)
    factor = jnp.where(bits[:, :, None] > 0.5, local[None], 1.0 - local[None])
    return factor[:, 0] * factor[:, 1] * factor[:, 2]


def element_forces(corner_disp, frame, tension, material):
    grads = shape_gradients()
    deform = (
        jnp.einsum("iae,aj->ije", corner_disp, grads, precision=highest)
        + jnp.eye(3, dtype=jnp.float32)[:, :, None]
    )
    cof = jnp.stack(
        [
            jnp.stack(
                [
                    deform[1, 1] * deform[2, 2] - deform[1, 2] * deform[2, 1],
                    deform[1, 2] * deform[2, 0] - deform[1, 0] * deform[2, 2],
                    deform[1, 0] * deform[2, 1] - deform[1, 1] * deform[2, 0],
                ],
                0,
            ),
            jnp.stack(
                [
                    deform[0, 2] * deform[2, 1] - deform[0, 1] * deform[2, 2],
                    deform[0, 0] * deform[2, 2] - deform[0, 2] * deform[2, 0],
                    deform[0, 1] * deform[2, 0] - deform[0, 0] * deform[2, 1],
                ],
                0,
            ),
            jnp.stack(
                [
                    deform[0, 1] * deform[1, 2] - deform[0, 2] * deform[1, 1],
                    deform[0, 2] * deform[1, 0] - deform[0, 0] * deform[1, 2],
                    deform[0, 0] * deform[1, 1] - deform[0, 1] * deform[1, 0],
                ],
                0,
            ),
        ],
        0,
    )
    volume = deform[0, 0] * cof[0, 0] + deform[0, 1] * cof[0, 1] + deform[0, 2] * cof[0, 2]
    inverse_t = cof / volume
    stretch = jnp.sum(deform * frame[None], axis=1)
    stress = (
        material[0] * (deform - inverse_t)
        + material[1] * jnp.log(volume) * inverse_t
        + material[2] * tension * stretch[:, None] * frame[None]
    )
    return jnp.einsum("ije,aj->iae", stress, grads, precision=highest)


def shards(
    states,
    active,
    fibre_index,
    fibre_angle,
    conduct,
    gate_half,
    gate_slope,
    gate_tau,
    conductance,
    reversal,
    block_elem,
    block_weight,
    node_disp,
    elem_node,
    elem_fibre,
    material,
):
    depth = lax.axis_size("gz")
    plane = lax.axis_size("gx") * lax.axis_size("gy")
    devices = plane * depth
    elem_count = elem_node.shape[1]
    node_count = node_disp.shape[1]
    size_x, size_y, size_z = (states.shape[1], states.shape[2], states.shape[3])
    flat_ids = block_elem.reshape(-1)
    block_count = flat_ids.shape[0]
    capacity = 2 * block_count // devices
    slot_count = devices * capacity
    owner = flat_ids // elem_count
    local = flat_ids % elem_count
    order = jnp.arange(block_count, dtype=jnp.int32)
    same_owner = (owner[:, None] == owner[None, :]) & (order[None, :] < order[:, None])
    rank = jnp.sum(same_owner.astype(jnp.int32), axis=1)
    slot = owner * capacity + rank
    send_ids = (
        jnp.full((slot_count,), -1, jnp.int32).at[slot].set(local).reshape(plane, depth, capacity)
    )
    got_ids = lax.all_to_all(
        lax.all_to_all(send_ids, ("gx", "gy"), split_axis=0, concat_axis=0, tiled=True),
        "gz",
        split_axis=1,
        concat_axis=1,
        tiled=True,
    ).reshape(-1)
    valid = got_ids >= 0
    asked = jnp.where(valid, got_ids, 0)
    asked_nodes = elem_node[:, asked]
    answer = node_disp[:, asked_nodes] * valid.astype(jnp.float32)
    answer = answer.reshape(24, plane, depth, capacity)
    returned = lax.all_to_all(
        lax.all_to_all(answer, ("gx", "gy"), split_axis=1, concat_axis=1, tiled=True),
        "gz",
        split_axis=2,
        concat_axis=2,
        tiled=True,
    ).reshape(3, 8, slot_count)
    block_disp = returned[:, :, slot]
    fine = jnp.einsum("cab,ap->cbp", block_disp, blend_weights(), precision=highest)
    blocks_x = size_x // SBX
    blocks_y = size_y // SBY
    blocks_z = size_z // SBZ
    fine_disp = (
        fine.reshape(3, blocks_x, blocks_y, blocks_z, SBX, SBY, SBZ)
        .transpose(0, 1, 4, 2, 5, 3, 6)
        .reshape(3, size_x, size_y, size_z)
    )
    looked = tile_lookup(fibre_index, fibre_angle, conduct)
    live_tile = (active > 0).astype(jnp.float32)
    tile_coef = coefficients(looked[:3], looked[3], looked[4], live_tile)
    live = expand(live_tile[None])[0]
    coef = expand(tile_coef)
    for step in range(FINE_STEPS):
        gates, vstar, calcium = ionic(
            states, live, gate_half, gate_slope, gate_tau, conductance, reversal
        )
        padded = padded_2(vstar, (("gx", 0), ("gy", 1), ("gz", 2)), 1)
        flux = fluxes(padded, coef)
        lap = divergence(padded_2(flux, (("gx", 1), ("gy", 2), ("gz", 3)), 1))
        states = jnp.concatenate([(vstar + live * lap)[None], gates, calcium[None]], 0)
    calcium = states[NSTATE - 1]
    tension = calcium * calcium / (calcium * calcium + tension_half)
    block_mean = (
        tension.reshape(blocks_x, SBX, blocks_y, SBY, blocks_z, SBZ)
        .mean(axis=(1, 3, 5))
        .reshape(-1)
    )
    block_value = block_weight.reshape(-1) * block_mean
    send_value = (
        jnp.zeros((slot_count,), jnp.float32)
        .at[slot]
        .set(block_value)
        .reshape(plane, depth, capacity)
    )
    got_value = lax.all_to_all(
        lax.all_to_all(send_value, ("gx", "gy"), split_axis=0, concat_axis=0, tiled=True),
        "gz",
        split_axis=1,
        concat_axis=1,
        tiled=True,
    ).reshape(-1)
    elem_tension = jax.ops.segment_sum(
        jnp.where(valid, got_value, 0.0), asked, num_segments=elem_count
    )
    corner_disp = node_disp[:, elem_node]
    labels = jnp.arange(fibre_angle.shape[1], dtype=jnp.int32)
    onehot = (elem_fibre[None, :] == labels[:, None]).astype(jnp.float32)
    table = fibre_frame(fibre_angle[0], fibre_angle[1])
    elem_frame = jnp.sum(table[:, :, None] * onehot[None], axis=1)
    force = element_forces(corner_disp, elem_frame, elem_tension, material)
    flat_nodes = elem_node.reshape(-1)
    node_residual = jnp.stack(
        [
            jax.ops.segment_sum(force[k].reshape(-1), flat_nodes, num_segments=node_count)
            for k in range(3)
        ],
        0,
    )
    return (states, fine_disp, node_residual)


def solution(mesh):
    in_specs = (
        P(None, "gx", "gy", "gz"),
        P("gx", "gy", "gz"),
        P("gx", "gy", "gz"),
        P(),
        P(),
        P(),
        P(),
        P(),
        P(),
        P(),
        P("gx", "gy", "gz"),
        P("gx", "gy", "gz"),
        P(None, ("gx", "gy", "gz")),
        P(None, ("gx", "gy", "gz")),
        P(("gx", "gy", "gz")),
        P(),
    )
    out_specs = (P(None, "gx", "gy", "gz"), P(None, "gx", "gy", "gz"), P(None, ("gx", "gy", "gz")))
    return jax.shard_map(shards, mesh=mesh, in_specs=in_specs, out_specs=out_specs, check_vma=False)
```

profile of v0, /device:TPU:0, one launch (start us, length us, event | category | flops | bytes accessed | tf_op | source)
XLA Modules:
  0.0 268.3 jit_solution(3350829469342161884)
XLA Ops:
  4.0 5.2 %all-to-all-start = ((s32[8,4,16]{2,1,0:T(4,128)}), s32[8,4,16]{2,1,0:T(4,128)S(1)}, u32[]{:S(2)}, u32[]{:S(2)}) async-start(s32[8,4,16]{2,1,0:T(4,128)} %reshape.1263), calls=%async_computation | async-start | bytes 32768 | tf_op jit(solution)/shard_map/all_to_all | solution.py:225
  11.8 4.5 %multiply_reduce_fusion.1 = (f32[16,16,128]{2,1,0:T(8,128)S(1)}, f32[17,16,16,128]{3,2,1,0:T(8,128)}) fusion(f32[17]{0:T(128)} %param.25, f32[16,16,128]{2,1,0:T(8,128)S(1)} %get-tuple-element.27, f32[17]{0:T(128)} %param.24, f32[17]{0:T(128)S(1)} %divide_exponential_fusion, f32[19,16,16,128]{3,2,1,0:T(8,128)} %param.16, f32[17]{0:T(128)} %param.22, f32[17]{0:T(128)} %param.21), kind=kLoop, calls=%fused_computation.13 | loop fusion | flops 6651904 | bytes 4718932 | tf_op jit(solution)/shard_map/reduce_sum | solution.py:85
  17.7 4.5 %collective-permute-start.1 = (f32[1,16,128]{2,1,0:T(8,128)S(1)}, f32[1,16,128]{2,1,0:T(8,128)S(1)}, u32[]{:S(2)}, u32[]{:S(2)}) collective-permute-start(f32[1,16,128]{2,1,0:T(8,128)S(1)} %get-tuple-element.52), channel_id=1, source_target_pairs={{0,16},{1,17},{2,18},{3,19},{4,20},{5,21},{6,22},{7,23},{8,24},{9,... | collective-permute-start | bytes 24584 | tf_op jit(solution)/shard_map/ppermute | solution.py:29
  23.8 7.6 %gather_fusion.3 = f32[2048,3]{1,0:T(8,128)} fusion(f32[3,512]{0,1:T(8,128)S(1)} %copy.175, s32[2048]{0:T(1024)S(1)} %broadcast_clamp_fusion.1), kind=kCustom, calls=%fused_computation.3 | custom fusion | bytes 57344 | tf_op jit(solution)/shard_map/gather | solution.py:290
  38.4 4.9 %all-to-all-start.1 = ((s32[4,1,128]{2,1,0:T(1,128)}), s32[4,1,128]{2,1,0:T(1,128)S(1)}, u32[]{:S(2)}, u32[]{:S(2)}) async-start(s32[4,1,128]{2,1,0:T(1,128)} %reshape.1380), calls=%async_computation.1 | async-start | bytes 4096 | tf_op jit(solution)/shard_map/all_to_all | solution.py:224
  44.6 3.0 %collective-permute-start.3 = (f32[18,1,128]{2,1,0:T(1,128)S(1)}, f32[18,1,128]{2,1,0:T(1,128)S(1)}, u32[]{:S(2)}, u32[]{:S(2)}) collective-permute-start(f32[18,1,128]{2,1,0:T(1,128)S(1)} %get-tuple-element.48), channel_id=1, source_target_pairs={{0,4},{4,8},{8,12},{1,5},{5,9},{9,13},{2,6},{6,10},{10,14},{3,7},{... | collective-permute-start | bytes 27656 | tf_op jit(solution)/shard_map/ppermute | solution.py:29
  66.1 4.6 %collective-permute-start.5 = (f32[18,18,1]{2,1,0:T(8,128)S(1)}, f32[18,18,1]{2,1,0:T(8,128)S(1)}, u32[]{:S(2)}, u32[]{:S(2)}) collective-permute-start(f32[18,18,1]{2,1,0:T(8,128)S(1)} %get-tuple-element.44), channel_id=1, source_target_pairs={{0,1},{1,2},{2,3},{4,5},{5,6},{6,7},{8,9},{9,10},{10,11},{12,13},{... | collective-permute-start | bytes 3896 | tf_op jit(solution)/shard_map/ppermute | solution.py:29
  83.9 3.2 %collective-permute-done.6 = f32[3,1,16,128]{3,2,1,0:T(8,128)} collective-permute-done((f32[3,1,16,128]{3,2,1,0:T(8,128)}, f32[3,1,16,128]{3,2,1,0:T(8,128)}, u32[]{:S(2)}, u32[]{:S(2)}) %collective-permute-start.6) | collective-permute-done | bytes 24608 | tf_op jit(solution)/shard_map/ppermute | solution.py:31
  98.9 4.1 %collective-permute-start.11 = (f32[3,18,18,1]{2,3,1,0:T(1,128)S(1)}, f32[3,18,18,1]{2,3,1,0:T(1,128)S(1)}, u32[]{:S(2)}, u32[]{:S(2)}) collective-permute-start(f32[3,18,18,1]{2,3,1,0:T(1,128)S(1)} %copy.202), channel_id=1, source_target_pairs={{0,1},{1,2},{2,3},{4,5},{5,6},{6,7},{8,9},{9,10},{10,11},{12,13},{... | collective-permute-start | bytes 11672 | tf_op jit(solution)/shard_map/ppermute | solution.py:29
  104.3 14.1 %gather_fusion.1 = f32[4096,3]{1,0:T(8,128)} fusion(f32[3,512]{0,1:T(8,128)S(1)} %copy.175, s32[4096]{0:T(1024)S(1)} %broadcast_clamp_fusion), kind=kCustom, calls=%fused_computation.1 | custom fusion | bytes 114688 | tf_op jit(solution)/shard_map/gather | solution.py:234
  132.5 5.0 %all-to-all-start.4 = ((f32[8,4,16]{2,1,0:T(4,128)}), f32[8,4,16]{2,1,0:T(4,128)S(1)}, u32[]{:S(2)}, u32[]{:S(2)}) async-start(f32[8,4,16]{2,1,0:T(4,128)} %reshape.1267), calls=%async_computation.4 | async-start | bytes 32768 | tf_op jit(solution)/shard_map/all_to_all | solution.py:281
  137.6 3.2 %multiply_reduce_fusion = (f32[16,16,128]{2,1,0:T(8,128)S(1)}, f32[17,16,16,128]{3,2,1,0:T(8,128)S(1)}) fusion(f32[16,16,128]{2,1,0:T(8,128)S(1)} %bitcast.161, f32[17]{0:T(128)S(1)} %copy-done.42, f32[17]{0:T(128)S(1)} %copy-done.43, f32[17]{0:T(128)S(1)} %copy-done.47, f32[17,16,16,128]{3,2,1,0:T(8,128)} %get-tuple-element.25, ...), kind=kLoop, calls=%fused_computation.11 | loop fusion | flops 7208960 | bytes 6947172 | tf_op jit(solution)/shard_map/reduce_sum | solution.py:85
  143.7 6.0 %all-to-all-start.5 = ((f32[4,1,128]{2,1,0:T(1,128)}), f32[4,1,128]{2,1,0:T(1,128)S(1)}, u32[]{:S(2)}, u32[]{:S(2)}) async-start(f32[4,1,128]{2,1,0:T(1,128)} %reshape.1386), calls=%async_computation.5 | async-start | bytes 4096 | tf_op jit(solution)/shard_map/all_to_all | solution.py:280
  151.0 4.5 %collective-permute-start.13 = (f32[1,16,128]{2,1,0:T(8,128)S(1)}, f32[1,16,128]{2,1,0:T(8,128)S(1)}, u32[]{:S(2)}, u32[]{:S(2)}) collective-permute-start(f32[1,16,128]{2,1,0:T(8,128)S(1)} %get-tuple-element.50), channel_id=1, source_target_pairs={{0,16},{1,17},{2,18},{3,19},{4,20},{5,21},{6,22},{7,23},{8,24},{9,... | collective-permute-start | bytes 24584 | tf_op jit(solution)/shard_map/ppermute | solution.py:29
  157.0 4.2 %scatter_custom_fusion.2 = f32[256]{0:T(256)S(1)} fusion(s32[512]{0:T(512)} %bitcast.190, f32[512]{0:T(512)S(1)} %reshape.1324, f32[]{:T(128)} %constant.159.clone.1), kind=kCustom, calls=%fused_computation.338 | custom fusion | flops 512 | bytes 1536 | tf_op jit(solution)/shard_map/scatter-add | solution.py:287
  163.2 3.0 %collective-permute-start.15 = (f32[18,1,128]{2,1,0:T(1,128)S(1)}, f32[18,1,128]{2,1,0:T(1,128)S(1)}, u32[]{:S(2)}, u32[]{:S(2)}) collective-permute-start(f32[18,1,128]{2,1,0:T(1,128)S(1)} %get-tuple-element.46), channel_id=1, source_target_pairs={{0,4},{4,8},{8,12},{1,5},{5,9},{9,13},{2,6},{6,10},{10,14},{3,7},{... | collective-permute-start | bytes 27656 | tf_op jit(solution)/shard_map/ppermute | solution.py:29
  168.5 4.6 %collective-permute-start.17 = (f32[18,18,1]{2,1,0:T(8,128)S(1)}, f32[18,18,1]{2,1,0:T(8,128)S(1)}, u32[]{:S(2)}, u32[]{:S(2)}) collective-permute-start(f32[18,18,1]{2,1,0:T(8,128)S(1)} %get-tuple-element.42), channel_id=1, source_target_pairs={{0,1},{1,2},{2,3},{4,5},{5,6},{6,7},{8,9},{9,10},{10,11},{12,13},{... | collective-permute-start | bytes 3896 | tf_op jit(solution)/shard_map/ppermute | solution.py:29
  178.6 4.1 %collective-permute-start.19 = (f32[3,1,16,128]{3,2,1,0:T(8,128)S(1)}, f32[3,1,16,128]{3,2,1,0:T(8,128)S(1)}, u32[]{:S(2)}, u32[]{:S(2)}) collective-permute-start(f32[3,1,16,128]{3,2,1,0:T(8,128)S(1)} %get-tuple-element.37), channel_id=1, source_target_pairs={{0,16},{1,17},{2,18},{3,19},{4,20},{5,21},{6,22},{7,23},{8,24},{9,... | collective-permute-start | bytes 73736 | tf_op jit(solution)/shard_map/ppermute | solution.py:29
  184.1 14.8 %scatter_custom_fusion.3 = f32[512]{0:T(512)S(1)} fusion(s32[2048]{0:T(1024)} %bitcast.180, f32[2048]{0:T(1024)S(1)} %bitcast.183, f32[]{:T(128)} %constant.159.clone.1), kind=kCustom, calls=%fused_computation.299 | custom fusion | flops 2048 | bytes 2560 | tf_op jit(solution)/shard_map/scatter-add | solution.py:299
  198.9 14.8 %scatter_custom_fusion.5 = f32[512]{0:T(512)S(1)} fusion(s32[2048]{0:T(1024)} %bitcast.181, f32[2048]{0:T(1024)S(1)} %bitcast.184, f32[]{:T(128)} %constant.159.clone.1), kind=kCustom, calls=%fused_computation.295 | custom fusion | flops 2048 | bytes 2560 | tf_op jit(solution)/shard_map/scatter-add | solution.py:299
  213.7 14.8 %scatter_custom_fusion.4 = f32[512]{0:T(512)S(1)} fusion(s32[2048]{0:T(1024)} %bitcast.182, f32[2048]{0:T(1024)S(1)} %bitcast.185, f32[]{:T(128)} %constant.159.clone.1), kind=kCustom, calls=%fused_computation.297 | custom fusion | flops 2048 | bytes 2560 | tf_op jit(solution)/shard_map/scatter-add | solution.py:299
  229.6 4.4 %all-to-all-start.2 = ((f32[8,1,1536]{2,1,0:T(1,128)}), f32[8,1,1536]{2,1,0:T(1,128)S(1)}, u32[]{:S(2)}, u32[]{:S(2)}) async-start(f32[8,1,1536]{2,1,0:T(1,128)} %reshape.1382), calls=%async_computation.2 | async-start | bytes 98304 | tf_op jit(solution)/shard_map/all_to_all | solution.py:237
  242.6 5.1 %collective-permute-start.23 = (f32[3,18,18,1]{2,3,1,0:T(1,128)}, f32[3,18,18,1]{2,3,1,0:T(1,128)}, u32[]{:S(2)}, u32[]{:S(2)}) collective-permute-start(f32[3,18,18,1]{2,3,1,0:T(1,128)} %copy.204), channel_id=1, source_target_pairs={{0,1},{1,2},{2,3},{4,5},{5,6},{6,7},{8,9},{9,10},{10,11},{12,13},{... | collective-permute-start | bytes 11672 | tf_op jit(solution)/shard_map/ppermute | solution.py:29
  249.8 4.8 %all-to-all-start.3 = ((f32[4,1,3072]{2,1,0:T(1,128)}), f32[4,1,3072]{2,1,0:T(1,128)}, u32[]{:S(2)}, u32[]{:S(2)}) async-start(f32[4,1,3072]{2,1,0:T(1,128)} %reshape.1384), calls=%async_computation.3 | async-start | bytes 98304 | tf_op jit(solution)/shard_map/all_to_all | solution.py:236
  (348 shorter events, 117.1 us)
Async XLA Ops:
  4.0 33.7 %all-to-all-start = ((s32[8,4,16]{2,1,0:T(4,128)}), s32[8,4,16]{2,1,0:T(4,128)S(1)}, u32[]{:S(2)}, u32[]{:S(2)}) async-start(s32[8,4,16]{2,1,0:T(4,128)} %reshape.1263), calls=%async_computation | async-start | bytes 32768 | tf_op jit(solution)/shard_map/all_to_all | solution.py:225
  16.4 26.8 %collective-permute-start = (f32[1,16,128]{2,1,0:T(8,128)S(1)}, f32[1,16,128]{2,1,0:T(8,128)S(1)}, u32[]{:S(2)}, u32[]{:S(2)}) collective-permute-start(f32[1,16,128]{2,1,0:T(8,128)S(1)} %get-tuple-element.51), channel_id=1, source_target_pairs={{16,0},{17,1},{18,2},{19,3},{20,4},{21,5},{22,6},{23,7},{24,8},{25... | collective-permute-start | bytes 24584 | tf_op jit(solution)/shard_map/ppermute | solution.py:31
  17.7 25.6 %collective-permute-start.1 = (f32[1,16,128]{2,1,0:T(8,128)S(1)}, f32[1,16,128]{2,1,0:T(8,128)S(1)}, u32[]{:S(2)}, u32[]{:S(2)}) collective-permute-start(f32[1,16,128]{2,1,0:T(8,128)S(1)} %get-tuple-element.52), channel_id=1, source_target_pairs={{0,16},{1,17},{2,18},{3,19},{4,20},{5,21},{6,22},{7,23},{8,24},{9,... | collective-permute-start | bytes 24584 | tf_op jit(solution)/shard_map/ppermute | solution.py:29
  38.4 24.3 %all-to-all-start.1 = ((s32[4,1,128]{2,1,0:T(1,128)}), s32[4,1,128]{2,1,0:T(1,128)S(1)}, u32[]{:S(2)}, u32[]{:S(2)}) async-start(s32[4,1,128]{2,1,0:T(1,128)} %reshape.1380), calls=%async_computation.1 | async-start | bytes 4096 | tf_op jit(solution)/shard_map/all_to_all | solution.py:224
  43.3 21.3 %collective-permute-start.2 = (f32[18,1,128]{2,1,0:T(1,128)S(1)}, f32[18,1,128]{2,1,0:T(1,128)S(1)}, u32[]{:S(2)}, u32[]{:S(2)}) collective-permute-start(f32[18,1,128]{2,1,0:T(1,128)S(1)} %get-tuple-element.47), channel_id=1, source_target_pairs={{4,0},{8,4},{12,8},{5,1},{9,5},{13,9},{6,2},{10,6},{14,10},{7,3},{... | collective-permute-start | bytes 27656 | tf_op jit(solution)/shard_map/ppermute | solution.py:31
  44.6 20.1 %collective-permute-start.3 = (f32[18,1,128]{2,1,0:T(1,128)S(1)}, f32[18,1,128]{2,1,0:T(1,128)S(1)}, u32[]{:S(2)}, u32[]{:S(2)}) collective-permute-start(f32[18,1,128]{2,1,0:T(1,128)S(1)} %get-tuple-element.48), channel_id=1, source_target_pairs={{0,4},{4,8},{8,12},{1,5},{5,9},{9,13},{2,6},{6,10},{10,14},{3,7},{... | collective-permute-start | bytes 27656 | tf_op jit(solution)/shard_map/ppermute | solution.py:29
  64.8 9.2 %collective-permute-start.4 = (f32[18,18,1]{2,1,0:T(8,128)S(1)}, f32[18,18,1]{2,1,0:T(8,128)S(1)}, u32[]{:S(2)}, u32[]{:S(2)}) collective-permute-start(f32[18,18,1]{2,1,0:T(8,128)S(1)} %get-tuple-element.43), channel_id=1, source_target_pairs={{1,0},{2,1},{3,2},{5,4},{6,5},{7,6},{9,8},{10,9},{11,10},{13,12},{... | collective-permute-start | bytes 3896 | tf_op jit(solution)/shard_map/ppermute | solution.py:31
  66.1 9.7 %collective-permute-start.5 = (f32[18,18,1]{2,1,0:T(8,128)S(1)}, f32[18,18,1]{2,1,0:T(8,128)S(1)}, u32[]{:S(2)}, u32[]{:S(2)}) collective-permute-start(f32[18,18,1]{2,1,0:T(8,128)S(1)} %get-tuple-element.44), channel_id=1, source_target_pairs={{0,1},{1,2},{2,3},{4,5},{5,6},{6,7},{8,9},{9,10},{10,11},{12,13},{... | collective-permute-start | bytes 3896 | tf_op jit(solution)/shard_map/ppermute | solution.py:29
  80.9 6.1 %collective-permute-start.6 = (f32[3,1,16,128]{3,2,1,0:T(8,128)}, f32[3,1,16,128]{3,2,1,0:T(8,128)}, u32[]{:S(2)}, u32[]{:S(2)}) collective-permute-start(f32[3,1,16,128]{3,2,1,0:T(8,128)} %get-tuple-element.40), channel_id=1, source_target_pairs={{16,0},{17,1},{18,2},{19,3},{20,4},{21,5},{22,6},{23,7},{24,8},{25... | collective-permute-start | bytes 73736 | tf_op jit(solution)/shard_map/ppermute | solution.py:31
  87.8 5.9 %collective-permute-start.9 = (f32[3,18,1,128]{3,2,1,0:T(1,128)S(1)}, f32[3,18,1,128]{3,2,1,0:T(1,128)S(1)}, u32[]{:S(2)}, u32[]{:S(2)}) collective-permute-start(f32[3,18,1,128]{3,2,1,0:T(1,128)S(1)} %get-tuple-element.35), channel_id=1, source_target_pairs={{0,4},{4,8},{8,12},{1,5},{5,9},{9,13},{2,6},{6,10},{10,14},{3,7},{... | collective-permute-start | bytes 82952 | tf_op jit(solution)/shard_map/ppermute | solution.py:29
  98.9 24.1 %collective-permute-start.11 = (f32[3,18,18,1]{2,3,1,0:T(1,128)S(1)}, f32[3,18,18,1]{2,3,1,0:T(1,128)S(1)}, u32[]{:S(2)}, u32[]{:S(2)}) collective-permute-start(f32[3,18,18,1]{2,3,1,0:T(1,128)S(1)} %copy.202), channel_id=1, source_target_pairs={{0,1},{1,2},{2,3},{4,5},{5,6},{6,7},{8,9},{9,10},{10,11},{12,13},{... | collective-permute-start | bytes 11672 | tf_op jit(solution)/shard_map/ppermute | solution.py:29
  103.0 18.7 %collective-permute-start.10 = (f32[3,18,18,1]{2,3,1,0:T(1,128)S(1)}, f32[3,18,18,1]{2,3,1,0:T(1,128)S(1)}, u32[]{:S(2)}, u32[]{:S(2)}) collective-permute-start(f32[3,18,18,1]{2,3,1,0:T(1,128)S(1)} %copy.201), channel_id=1, source_target_pairs={{1,0},{2,1},{3,2},{5,4},{6,5},{7,6},{9,8},{10,9},{11,10},{13,12},{... | collective-permute-start | bytes 11672 | tf_op jit(solution)/shard_map/ppermute | solution.py:31
  132.5 10.5 %all-to-all-start.4 = ((f32[8,4,16]{2,1,0:T(4,128)}), f32[8,4,16]{2,1,0:T(4,128)S(1)}, u32[]{:S(2)}, u32[]{:S(2)}) async-start(f32[8,4,16]{2,1,0:T(4,128)} %reshape.1267), calls=%async_computation.4 | async-start | bytes 32768 | tf_op jit(solution)/shard_map/all_to_all | solution.py:281
  143.7 11.8 %all-to-all-start.5 = ((f32[4,1,128]{2,1,0:T(1,128)}), f32[4,1,128]{2,1,0:T(1,128)S(1)}, u32[]{:S(2)}, u32[]{:S(2)}) async-start(f32[4,1,128]{2,1,0:T(1,128)} %reshape.1386), calls=%async_computation.5 | async-start | bytes 4096 | tf_op jit(solution)/shard_map/all_to_all | solution.py:280
  149.7 12.1 %collective-permute-start.12 = (f32[1,16,128]{2,1,0:T(8,128)S(1)}, f32[1,16,128]{2,1,0:T(8,128)S(1)}, u32[]{:S(2)}, u32[]{:S(2)}) collective-permute-start(f32[1,16,128]{2,1,0:T(8,128)S(1)} %get-tuple-element.49), channel_id=1, source_target_pairs={{16,0},{17,1},{18,2},{19,3},{20,4},{21,5},{22,6},{23,7},{24,8},{25... | collective-permute-start | bytes 24584 | tf_op jit(solution)/shard_map/ppermute | solution.py:31
  151.0 10.8 %collective-permute-start.13 = (f32[1,16,128]{2,1,0:T(8,128)S(1)}, f32[1,16,128]{2,1,0:T(8,128)S(1)}, u32[]{:S(2)}, u32[]{:S(2)}) collective-permute-start(f32[1,16,128]{2,1,0:T(8,128)S(1)} %get-tuple-element.50), channel_id=1, source_target_pairs={{0,16},{1,17},{2,18},{3,19},{4,20},{5,21},{6,22},{7,23},{8,24},{9,... | collective-permute-start | bytes 24584 | tf_op jit(solution)/shard_map/ppermute | solution.py:29
  167.2 9.1 %collective-permute-start.16 = (f32[18,18,1]{2,1,0:T(8,128)S(1)}, f32[18,18,1]{2,1,0:T(8,128)S(1)}, u32[]{:S(2)}, u32[]{:S(2)}) collective-permute-start(f32[18,18,1]{2,1,0:T(8,128)S(1)} %get-tuple-element.41), channel_id=1, source_target_pairs={{1,0},{2,1},{3,2},{5,4},{6,5},{7,6},{9,8},{10,9},{11,10},{13,12},{... | collective-permute-start | bytes 3896 | tf_op jit(solution)/shard_map/ppermute | solution.py:31
  168.5 9.6 %collective-permute-start.17 = (f32[18,18,1]{2,1,0:T(8,128)S(1)}, f32[18,18,1]{2,1,0:T(8,128)S(1)}, u32[]{:S(2)}, u32[]{:S(2)}) collective-permute-start(f32[18,18,1]{2,1,0:T(8,128)S(1)} %get-tuple-element.42), channel_id=1, source_target_pairs={{0,1},{1,2},{2,3},{4,5},{5,6},{6,7},{8,9},{9,10},{10,11},{12,13},{... | collective-permute-start | bytes 3896 | tf_op jit(solution)/shard_map/ppermute | solution.py:29
  178.6 55.4 %collective-permute-start.19 = (f32[3,1,16,128]{3,2,1,0:T(8,128)S(1)}, f32[3,1,16,128]{3,2,1,0:T(8,128)S(1)}, u32[]{:S(2)}, u32[]{:S(2)}) collective-permute-start(f32[3,1,16,128]{3,2,1,0:T(8,128)S(1)} %get-tuple-element.37), channel_id=1, source_target_pairs={{0,16},{1,17},{2,18},{3,19},{4,20},{5,21},{6,22},{7,23},{8,24},{9,... | collective-permute-start | bytes 73736 | tf_op jit(solution)/shard_map/ppermute | solution.py:29
  182.7 51.3 %collective-permute-start.18 = (f32[3,1,16,128]{3,2,1,0:T(8,128)S(1)}, f32[3,1,16,128]{3,2,1,0:T(8,128)S(1)}, u32[]{:S(2)}, u32[]{:S(2)}) collective-permute-start(f32[3,1,16,128]{3,2,1,0:T(8,128)S(1)} %get-tuple-element.38), channel_id=1, source_target_pairs={{16,0},{17,1},{18,2},{19,3},{20,4},{21,5},{22,6},{23,7},{24,8},{25... | collective-permute-start | bytes 73736 | tf_op jit(solution)/shard_map/ppermute | solution.py:31
  229.6 9.2 %all-to-all-start.2 = ((f32[8,1,1536]{2,1,0:T(1,128)}), f32[8,1,1536]{2,1,0:T(1,128)S(1)}, u32[]{:S(2)}, u32[]{:S(2)}) async-start(f32[8,1,1536]{2,1,0:T(1,128)} %reshape.1382), calls=%async_computation.2 | async-start | bytes 98304 | tf_op jit(solution)/shard_map/all_to_all | solution.py:237
  242.6 13.3 %collective-permute-start.23 = (f32[3,18,18,1]{2,3,1,0:T(1,128)}, f32[3,18,18,1]{2,3,1,0:T(1,128)}, u32[]{:S(2)}, u32[]{:S(2)}) collective-permute-start(f32[3,18,18,1]{2,3,1,0:T(1,128)} %copy.204), channel_id=1, source_target_pairs={{0,1},{1,2},{2,3},{4,5},{5,6},{6,7},{8,9},{9,10},{10,11},{12,13},{... | collective-permute-start | bytes 11672 | tf_op jit(solution)/shard_map/ppermute | solution.py:29
  247.7 7.0 %collective-permute-start.22 = (f32[3,18,18,1]{2,3,1,0:T(1,128)S(1)}, f32[3,18,18,1]{2,3,1,0:T(1,128)}, u32[]{:S(2)}, u32[]{:S(2)}) collective-permute-start(f32[3,18,18,1]{2,3,1,0:T(1,128)S(1)} %copy.203), channel_id=1, source_target_pairs={{1,0},{2,1},{3,2},{5,4},{6,5},{7,6},{9,8},{10,9},{11,10},{13,12},{... | collective-permute-start | bytes 11672 | tf_op jit(solution)/shard_map/ppermute | solution.py:31
  249.8 11.1 %all-to-all-start.3 = ((f32[4,1,3072]{2,1,0:T(1,128)}), f32[4,1,3072]{2,1,0:T(1,128)}, u32[]{:S(2)}, u32[]{:S(2)}) async-start(f32[4,1,3072]{2,1,0:T(1,128)} %reshape.1384), calls=%async_computation.3 | async-start | bytes 98304 | tf_op jit(solution)/shard_map/all_to_all | solution.py:236
  (72 other events, 1088.3 us)
where the time goes:
time: 272 us; the launch traced here: 268 us
  starting transfers between devices  89.5 us (33%)
  other arithmetic  85.4 us (31%)
  local copies, waits for them, and re-layouts  75 us (28%)
  waiting for transfers between devices  13.2 us (5%)
  matrix products  3.02 us (1%)
    scatter-add x3, other arithmetic, shards(): jax.ops.segment_sum(force[k].reshape(-1), flat_nodes, num_segments=node_c...  44.4 us
    ppermute x12, starting transfers between devices, padded_2(): lax.ppermute(tail, axis, [(i, (i + 1) % count) for i in range(ends)])  43.7 us
    gather x3, local copies, waits for them, and re-layouts, shards(): answer = node_disp[:, asked_nodes] * valid.astype(jnp.float32)  17.4 us
    ppermute x12, starting transfers between devices, padded_2(): lax.ppermute(head, axis, [((i + 1) % count, i) for i in range(ends)])  15.5 us
    unnamed x156, local copies, waits for them, and re-layouts  11.4 us
    gather x2, local copies, waits for them, and re-layouts, shards(): corner_disp = node_disp[:, elem_node]  9.13 us
    ppermute x12, waiting for transfers between devices, padded_2(): lax.ppermute(head, axis, [((i + 1) % count, i) for i in range(ends)])  8.53 us
    reduce_sum x2, other arithmetic, ionic(): jnp.sum(conductance.reshape(shape) * gates * (volt[None] - reversal.resha...  7.67 us
  transfers between devices with their start and end apart: 30, of which 8 were waited for; matrix products, arithmetic and copies ran while one was open for 49% of the time, Pallas kernels for 0%

commit v1 on v0

v1 whole, which is shorter than its diff:
```python
import functools

import jax
import jax.numpy as jnp
from jax import lax
from jax.experimental import pallas as pl
from jax.experimental.pallas import tpu as pltpu
from jax.sharding import PartitionSpec as P

NSTATE = 19
TLX = 8
SBX = 2
SBY = 2
SBZ = 32
FINE_STEPS = 2
AXES = ("gx", "gy", "gz")
MESH = pl.DeviceIdType.MESH
LANES = 128
f32 = jnp.float32
bf16 = jnp.bfloat16
calcium_keep = 0.9
tension_half = 0.09
NN = (((1,), (0,)), ((), ()))
NT = (((1,), (1,)), ((), ()))


def mm(a, b, dims=NN):
    return lax.dot_general(a, b, dims, preferred_element_type=f32)


def parts3(x):
    x1 = x.astype(bf16)
    r1 = x - x1.astype(f32)
    x2 = r1.astype(bf16)
    x3 = (r1 - x2.astype(f32)).astype(bf16)
    return x1, x2, x3


def rows3(x):
    return jnp.concatenate([p.astype(f32) for p in parts3(x)], 0).astype(bf16)


def fold3(y):
    r = y.shape[0] // 3
    return y[:r] + y[r : 2 * r] + y[2 * r :]


def mm_right3(a, x, dims=NN):
    x1, x2, x3 = parts3(x)
    return mm(a, x1, dims) + mm(a, x2, dims) + mm(a, x3, dims)


def iota(shape, dim):
    return lax.broadcasted_iota(jnp.int32, shape, dim)


def column(row):
    pieces = [
        jnp.transpose(jnp.broadcast_to(row[:, i : i + LANES], (LANES, LANES)))
        for i in range(0, row.shape[1], LANES)
    ]
    return pieces[0] if len(pieces) == 1 else jnp.concatenate(pieces, 0)


def onehot(mask):
    return jnp.where(mask, 1.0, 0.0).astype(bf16)


def pick_rows(rows, shape):
    index = iota(shape, 0)
    out = jnp.zeros(shape, f32)
    for i, row in enumerate(rows):
        out = jnp.where(index == i, row, out)
    return out


def sigmoid(u):
    return 0.5 * jnp.tanh(0.5 * u) + 0.5


def frame_of(a, b):
    return jnp.cos(a) * jnp.cos(b), jnp.sin(a) * jnp.cos(b), jnp.sin(b)


def body(
    sizes,
    states,
    active,
    fibre_index,
    angle_s,
    angle_v,
    conduct,
    gate_half,
    gate_slope,
    gate_tau,
    conductance,
    reversal,
    ids_ref,
    weight_ref,
    node_disp,
    elem_node,
    elem_fibre,
    material,
    out,
    fine_out,
    resid_out,
    vs,
    flux,
    send_y,
    send_z,
    halo_x,
    halo_y,
    halo_z,
    corner_oh,
    corner_cd,
    slot_oh,
    pick_oh,
    owner_oh,
    rank_oh,
    ids_send,
    ids_got,
    val_send,
    val_got,
    ans_send,
    ans_got,
    face_send_sem,
    face_recv_sem,
    all_send_sem,
    all_recv_sem,
):
    mx, my, mz, seats, elem_count = sizes
    n = mx * my * mz
    nx, ny, nz = states.shape[1:]
    gates_n = NSTATE - 2
    bx, by, bz = nx // SBX, ny // SBY, nz // SBZ
    plane = bx * by
    blocks = plane * bz
    slots = n * seats
    tiles = nx // TLX
    node_count = node_disp.shape[1]
    corners = 8
    cx, cy, cz = (lax.axis_index(a) for a in AXES)
    me = (cx * my + cy) * mz + cz

    def coords(flat):
        return flat // (my * mz), (flat // mz) % my, flat % mz

    barrier = pltpu.get_barrier_semaphore()

    def greet(k, carry):
        pl.semaphore_signal(
            barrier, inc=1, device_id=coords((me + k) % n), device_id_type=MESH
        )
        return carry

    lax.fori_loop(1, n, greet, 0)

    def splat(value):
        return jnp.full((1, 1, LANES), value, f32)

    coef, live = [], []
    for t in range(tiles):
        index = fibre_index[t, 0, 0]
        fx, fy, fz = frame_of(splat(angle_s[0, index]), splat(angle_s[1, index]))
        across = splat(conduct[1, index])
        spread = splat(conduct[0, index]) - across
        alive = splat(jnp.where(active[t, 0, 0] > 0, 1.0, 0.0).astype(f32))
        live.append(alive)
        coef.append(
            [
                (across + spread * fx * fx) * alive,
                (across + spread * fy * fy) * alive,
                (across + spread * fz * fz) * alive,
                spread * fx * fy * alive,
                spread * fx * fz * alive,
                spread * fy * fz * alive,
            ]
        )

    chunk = 4

    def ionic(source, t):
        alive = live[t] > 0.5

        def step(i, carry):
            at = pl.ds(t * TLX + i * chunk, chunk)
            volt = source[0, at]
            current = jnp.zeros_like(volt)
            for g in range(gates_n):
                inv = 1.0 / splat(gate_slope[g])
                keep = jnp.exp(-1.0 / splat(gate_tau[g]))
                steady = sigmoid((volt - splat(gate_half[g])) * inv)
                old = source[1 + g, at]
                gate = steady + (old - steady) * keep
                current = current + splat(conductance[g]) * gate * (volt - splat(reversal[g]))
                out[1 + g, at] = jnp.where(alive, gate, old)
            old = source[NSTATE - 1, at]
            calcium = old * calcium_keep + (1.0 - calcium_keep) * sigmoid(8.0 * (volt - 0.5))
            out[NSTATE - 1, at] = jnp.where(alive, calcium, old)
            vs[at] = jnp.where(alive, volt - current, volt)
            return carry

        lax.fori_loop(0, TLX // chunk, step, 0)

    def face_copies(stage, low_x, high_x):
        near = [(cx, mx), (cy, my), (cz, mz)]
        made = []
        for dim in range(3):
            for side in range(2):
                if dim == 0:
                    src = high_x if side == 0 else low_x
                    dst = halo_x.at[stage, side]
                elif dim == 1:
                    src, dst = send_y.at[stage, side], halo_y.at[stage, side]
                else:
                    src, dst = send_z.at[stage, side], halo_z.at[stage, side]
                at, count = near[dim]
                to = [cx, cy, cz]
                to[dim] = (at + (1 if side == 0 else count - 1)) % count
                made.append(
                    pltpu.make_async_remote_copy(
                        src_ref=src,
                        dst_ref=dst,
                        send_sem=face_send_sem.at[stage, 2 * dim + side],
                        recv_sem=face_recv_sem.at[stage, 2 * dim + side],
                        device_id=tuple(to),
                        device_id_type=MESH,
                    )
                )
        return made

    def flat_z(a):
        return jnp.transpose(a.reshape(nx * ny, nz))

    def send_faces(stage, a_y, a_z, low_x, high_x):
        send_y[stage, 0] = a_y[:, ny - 1 : ny, :]
        send_y[stage, 1] = a_y[:, 0:1, :]
        turned = flat_z(a_z)
        send_z[stage, 0] = turned[nz - 1 : nz, :]
        send_z[stage, 1] = turned[0:1, :]
        copies = face_copies(stage, low_x, high_x)
        for c in copies:
            c.start()
        return copies

    def masked(value, inside):
        return jnp.where(inside, value, 0.0)

    def diff_x(a, stage):
        low = masked(halo_x[stage, 0], cx > 0)[None]
        high = masked(halo_x[stage, 1], cx < mx - 1)[None]
        up = jnp.concatenate([a[1:], high], 0)
        down = jnp.concatenate([low, a[:-1]], 0)
        return (up - down) * 0.5

    def diff_y(a, stage):
        low = masked(halo_y[stage, 0], cy > 0)
        high = masked(halo_y[stage, 1], cy < my - 1)
        row = iota((1, ny, nz), 1)
        down = jnp.where(row == 0, low, pltpu.roll(a, 1, 1))
        up = jnp.where(row == ny - 1, high, pltpu.roll(a, ny - 1, 1))
        return (up - down) * 0.5

    def diff_z(a, stage):
        low = masked(halo_z[stage, 0], cz > 0)
        high = masked(halo_z[stage, 1], cz < mz - 1)
        row = iota((nz, nx * ny), 0)
        edge = jnp.where(row == 0, low, jnp.where(row == nz - 1, high, 0.0))
        edge = jnp.transpose(edge).reshape(nx, ny, nz)
        lane = iota((1, 1, nz), 2)
        down = jnp.where(lane == 0, edge, pltpu.roll(a, 1, 2))
        up = jnp.where(lane == nz - 1, edge, pltpu.roll(a, nz - 1, 2))
        return (up - down) * 0.5

    def make_flux(stage):
        v = vs[...]
        gx, gy, gz = diff_x(v, stage), diff_y(v, stage), diff_z(v, stage)
        for t in range(tiles):
            at = slice(t * TLX, (t + 1) * TLX)
            xx, yy, zz, xy, xz, yz = coef[t]
            a, b, c = gx[at], gy[at], gz[at]
            flux[0, at] = xx * a + xy * b + xz * c
            flux[1, at] = xy * a + yy * b + yz * c
            flux[2, at] = xz * a + yz * b + zz * c

    def finish(stage):
        lap = diff_x(flux[0], stage) + diff_y(flux[1], stage) + diff_z(flux[2], stage)
        for t in range(tiles):
            at = slice(t * TLX, (t + 1) * TLX)
            out[0, at] = vs[at] + live[t] * lap[at]

    def all_copy(k, kind, src, dst):
        return pltpu.make_async_remote_copy(
            src_ref=src.at[(me + k) % n],
            dst_ref=dst.at[me],
            send_sem=all_send_sem.at[kind, k],
            recv_sem=all_recv_sem.at[kind, k],
            device_id=coords((me + k) % n),
            device_id_type=MESH,
        )

    def all_start(kind, src, dst):
        dst[pl.ds(me, 1)] = src[pl.ds(me, 1)]

        def go(k, carry):
            all_copy(k, kind, src, dst).start()
            return carry

        lax.fori_loop(1, n, go, 0)

    def all_wait(kind, src, dst):
        def go(k, carry):
            pltpu.make_async_remote_copy(
                src_ref=src.at[(me + k) % n],
                dst_ref=dst.at[(me + n - k) % n],
                send_sem=all_send_sem.at[kind, k],
                recv_sem=all_recv_sem.at[kind, k],
                device_id=coords((me + k) % n),
                device_id_type=MESH,
            ).wait()
            return carry

        lax.fori_loop(1, n, go, 0)

    per_row = LANES // seats
    groups = slots // LANES

    def lanes_of(got):
        pieces = []
        for g in range(groups):
            pieces.append(
                lax.fori_loop(
                    0,
                    per_row,
                    lambda r, acc, g=g: acc + got[g * per_row + r],
                    jnp.zeros((1, LANES), f32),
                )
            )
        return jnp.concatenate(pieces, 1)

    for t in range(tiles):
        ionic(states, t)
    shift = elem_count.bit_length() - 1
    ids = ids_ref[...]
    owner = lax.shift_right_logical(ids, shift)
    local = ids - owner * elem_count
    owner_col = column(owner.astype(f32))
    owner_f = owner.astype(f32)
    owner_cols = jnp.concatenate([owner_col] * (blocks // LANES), 1)
    earlier = (owner_cols == owner_f) & (iota((blocks, blocks), 1) < iota((blocks, blocks), 0))
    rank = jnp.sum(jnp.where(earlier, 1.0, 0.0), axis=1, keepdims=True)
    offset = ((me % per_row) * seats).astype(f32)
    rank_hit = onehot(iota((blocks, LANES), 1).astype(f32) == rank + offset)
    rank_oh[...] = rank_hit
    owned = owner == iota((n, blocks), 0)
    owner_oh[...] = onehot(owned)
    slot_col = owner_col[:, 0:1] * seats + rank
    slot_oh[...] = onehot(iota((blocks, slots), 1).astype(f32) == slot_col)
    wanted = jnp.where(owned, local.astype(f32) + 1.0, 0.0).astype(bf16)
    ids_send[...] = mm(wanted, rank_hit).reshape(n, 1, LANES)

    pl.semaphore_wait(barrier, n - 1)
    v0 = vs[...]
    stage0 = send_faces(0, v0, v0, vs.at[0], vs.at[nx - 1])
    all_start(0, ids_send, ids_got)

    nodes = pick_rows([node_disp[i : i + 1, :] for i in range(3)], (8, node_count))
    nodes3 = rows3(nodes)
    for q in range(corners):
        hit = onehot(iota((node_count, elem_count), 0) == elem_node[q : q + 1, :])
        corner_oh[q] = hit
        corner_cd[q] = fold3(mm(nodes3, hit))

    for c in stage0:
        c.wait()
    make_flux(0)
    stage1 = send_faces(1, flux[1], flux[2], flux.at[0, 0], flux.at[0, nx - 1])

    all_wait(0, ids_send, ids_got)
    asked = column(lanes_of(ids_got)) - 1.0
    asked = jnp.concatenate([asked] * (elem_count // LANES), 1)
    pick_oh[...] = onehot(iota((slots, elem_count), 1).astype(f32) == asked)
    table = jnp.concatenate(
        [corner_cd[...].reshape(corners * 8, elem_count), jnp.zeros((LANES - corners * 8, elem_count), f32)],
        0,
    )
    ans_send[...] = mm_right3(pick_oh[...], table, NT).reshape(n, seats, LANES)
    all_start(1, ans_send, ans_got)

    for c in stage1:
        c.wait()
    finish(1)
    for t in range(tiles):
        ionic(out, t)
    v1 = vs[...]
    stage2 = send_faces(2, v1, v1, vs.at[0], vs.at[nx - 1])

    calcium = out[NSTATE - 1]
    square = calcium * calcium
    pull = (square / (square + tension_half)).reshape(bx, SBX, ny, nz)
    pull = (pull[:, 0] + pull[:, 1]).reshape(bx * ny, nz)
    pair = onehot(iota((plane, bx * ny), 1) // SBY == iota((plane, bx * ny), 0))
    pooled = mm_right3(pair, pull)
    strip = onehot(iota((nz, LANES), 0) // SBZ == iota((nz, LANES), 1))
    pooled = fold3(mm(rows3(pooled), strip)) * (1.0 / (SBX * SBY * SBZ))
    worth = jnp.concatenate(
        [
            jnp.broadcast_to(pooled[:, b : b + 1] * weight_ref[:, b : b + 1], (plane, LANES))
            for b in range(bz)
        ],
        0,
    )
    worth = jnp.where(rank_oh[...].astype(f32) > 0.5, worth, 0.0)
    val_send[...] = mm_right3(owner_oh[...], worth).reshape(n, 1, LANES)
    all_start(2, val_send, val_got)

    angle = angle_v[...]
    fx, fy, fz = frame_of(angle[0:1, :], angle[1:2, :])
    entries = angle.shape[1]
    fibres = pick_rows([fx, fy, fz], (8, entries))
    which = onehot(iota((entries, elem_count), 0) == elem_fibre[...])
    frames = fold3(mm(rows3(fibres), which))
    frame = [frames[i : i + 1, :] for i in range(3)]
    grads = [
        [((2 * (q // 4) - 1) / 4), ((2 * (q // 2 % 2) - 1) / 4), ((2 * (q % 2) - 1) / 4)]
        for q in range(corners)
    ]
    sums = [sum(corner_cd[q] * grads[q][j] for q in range(corners)) for j in range(3)]
    d = [
        [sums[j][i : i + 1, :] + (1.0 if i == j else 0.0) for j in range(3)] for i in range(3)
    ]
    cof = [
        [
            d[(i + 1) % 3][(j + 1) % 3] * d[(i + 2) % 3][(j + 2) % 3]
            - d[(i + 1) % 3][(j + 2) % 3] * d[(i + 2) % 3][(j + 1) % 3]
            for j in range(3)
        ]
        for i in range(3)
    ]
    volume = d[0][0] * cof[0][0] + d[0][1] * cof[0][1] + d[0][2] * cof[0][2]
    inverse = 1.0 / volume
    logv = jnp.log(volume)
    shear, bulk, scale = material[0], material[1], material[2]
    passive = [
        [
            shear * (d[i][j] - cof[i][j] * inverse) + bulk * logv * (cof[i][j] * inverse)
            for j in range(3)
        ]
        for i in range(3)
    ]
    stretch = [
        scale * (d[i][0] * frame[0] + d[i][1] * frame[1] + d[i][2] * frame[2]) for i in range(3)
    ]

    for c in stage2:
        c.wait()
    make_flux(2)
    stage3 = send_faces(3, flux[1], flux[2], flux.at[0, 0], flux.at[0, nx - 1])

    all_wait(1, ans_send, ans_got)
    returned = ans_got[...].reshape(slots, LANES)
    near = mm_right3(slot_oh[...], returned)
    lane = iota((plane, nz), 1)
    strip_of = lane // SBZ
    xi = ((lane % SBZ).astype(f32) + 0.5) / SBZ
    for c in range(3):
        lines = []
        for ij in range(4):
            ends = []
            for k in range(2):
                col = (2 * ij + k) * 8 + c
                value = jnp.zeros((plane, nz), f32)
                for b in range(bz):
                    value = jnp.where(
                        strip_of == b, near[b * plane : (b + 1) * plane, col : col + 1], value
                    )
                ends.append(value)
            lines.append(ends[0] * (1.0 - xi) + ends[1] * xi)
        for iv in range(SBX):
            wx = (iv + 0.5) / SBX
            for jv in range(SBY):
                wy = (jv + 0.5) / SBY
                value = (
                    lines[0] * ((1 - wx) * (1 - wy))
                    + lines[1] * ((1 - wx) * wy)
                    + lines[2] * (wx * (1 - wy))
                    + lines[3] * (wx * wy)
                )
                for p in range(bx):
                    fine_out[c, SBX * p + iv, pl.ds(jv, by, stride=SBY), :] = value[
                        p * by : (p + 1) * by
                    ]

    for c in stage3:
        c.wait()
    finish(3)

    all_wait(2, val_send, val_got)
    arrived = jnp.broadcast_to(lanes_of(val_got), (8, slots))
    tension = fold3(mm(rows3(arrived), pick_oh[...]))[0:1, :]
    total = jnp.zeros((24, node_count), f32)
    stress = [
        [passive[i][j] + tension * stretch[i] * frame[j] for j in range(3)] for i in range(3)
    ]
    for q in range(corners):
        force = pick_rows(
            [
                stress[i][0] * grads[q][0] + stress[i][1] * grads[q][1] + stress[i][2] * grads[q][2]
                for i in range(3)
            ],
            (8, elem_count),
        )
        total = total + mm(rows3(force), corner_oh[q], NT)
    resid_out[...] = fold3(total)[0:3, :]


def shards(
    states,
    active,
    fibre_index,
    fibre_angle,
    conduct,
    gate_half,
    gate_slope,
    gate_tau,
    conductance,
    reversal,
    block_elem,
    block_weight,
    node_disp,
    elem_node,
    elem_fibre,
    material,
):
    mx, my, mz = (lax.axis_size(a) for a in AXES)
    n = mx * my * mz
    elem_count = elem_node.shape[1]
    node_count = node_disp.shape[1]
    nx, ny, nz = states.shape[1:]
    bx, by, bz = block_elem.shape
    blocks = bx * by * bz
    seats = max(2 * blocks // n, 8)
    slots = n * seats
    ids = block_elem.transpose(2, 0, 1).reshape(1, blocks)
    weight = block_weight.reshape(bx * by, bz)
    vmem = pl.BlockSpec(memory_space=pltpu.VMEM)
    smem = pl.BlockSpec(memory_space=pltpu.SMEM)
    stages = 2 * FINE_STEPS
    return pl.pallas_call(
        functools.partial(body, (mx, my, mz, seats, elem_count)),
        out_shape=(
            jax.ShapeDtypeStruct(states.shape, f32),
            jax.ShapeDtypeStruct((3, nx, ny, nz), f32),
            jax.ShapeDtypeStruct((3, node_count), f32),
        ),
        in_specs=[vmem, smem, smem, smem, vmem] + [smem] * 6 + [vmem] * 5 + [smem],
        out_specs=(vmem, vmem, vmem),
        scratch_shapes=[
            pltpu.VMEM((nx, ny, nz), f32),
            pltpu.VMEM((3, nx, ny, nz), f32),
            pltpu.VMEM((stages, 2, nx, 1, nz), f32),
            pltpu.VMEM((stages, 2, 1, nx * ny), f32),
            pltpu.VMEM((stages, 2, ny, nz), f32),
            pltpu.VMEM((stages, 2, nx, 1, nz), f32),
            pltpu.VMEM((stages, 2, 1, nx * ny), f32),
            pltpu.VMEM((8, node_count, elem_count), bf16),
            pltpu.VMEM((8, 8, elem_count), f32),
            pltpu.VMEM((blocks, slots), bf16),
            pltpu.VMEM((slots, elem_count), bf16),
            pltpu.VMEM((n, blocks), bf16),
            pltpu.VMEM((blocks, LANES), bf16),
            pltpu.VMEM((n, 1, LANES), f32),
            pltpu.VMEM((n, 1, LANES), f32),
            pltpu.VMEM((n, 1, LANES), f32),
            pltpu.VMEM((n, 1, LANES), f32),
            pltpu.VMEM((n, seats, LANES), f32),
            pltpu.VMEM((n, seats, LANES), f32),
            pltpu.SemaphoreType.DMA((stages, 6)),
            pltpu.SemaphoreType.DMA((stages, 6)),
            pltpu.SemaphoreType.DMA((3, n)),
            pltpu.SemaphoreType.DMA((3, n)),
        ],
        compiler_params=pltpu.CompilerParams(
            collective_id=0, has_side_effects=True, vmem_limit_bytes=60 * 1024 * 1024
        ),
        name="step",
    )(
        states,
        active,
        fibre_index,
        fibre_angle,
        fibre_angle,
        conduct,
        gate_half,
        gate_slope,
        gate_tau,
        conductance,
        reversal,
        ids,
        weight,
        node_disp,
        elem_node,
        elem_fibre.reshape(1, elem_count),
        material,
    )


def solution(mesh):
    in_specs = (
        P(None, "gx", "gy", "gz"),
        P("gx", "gy", "gz"),
        P("gx", "gy", "gz"),
        P(),
        P(),
        P(),
        P(),
        P(),
        P(),
        P(),
        P("gx", "gy", "gz"),
        P("gx", "gy", "gz"),
        P(None, ("gx", "gy", "gz")),
        P(None, ("gx", "gy", "gz")),
        P(("gx", "gy", "gz")),
        P(),
    )
    out_specs = (P(None, "gx", "gy", "gz"), P(None, "gx", "gy", "gz"), P(None, ("gx", "gy", "gz")))
    return jax.shard_map(shards, mesh=mesh, in_specs=in_specs, out_specs=out_specs, check_vma=False)
```

time: 272 us -> 40.8 us (0.15); the launches traced: 268 us -> 40.5 us
  starting transfers between devices: 89.5 us -> 0 us
  other arithmetic: 85.4 us -> 0 us
  local copies, waits for them, and re-layouts: 75 us -> 10.1 us
  Pallas kernels: 0 us -> 29.7 us
  waiting for transfers between devices: 13.2 us -> 0 us
  matrix products: 3.02 us -> 0 us
    ppermute x24 -> x0, starting transfers between devices: 59.2 us -> none  [the longest x12 43.7 us: padded_2(): lax.ppermute(tail, axis, [(i, (i + 1) % count) for i in range(ends)])]
    scatter-add x4 -> x0, other arithmetic: 48.6 us -> none  [the longest x3 44.4 us: shards(): jax.ops.segment_sum(force[k].reshape(-1), flat_nodes, num_segments=node_c...]
    all_to_all x6 -> x0, starting transfers between devices: 30.3 us -> none  [the longest x1 5.99 us: shards(): lax.all_to_all(lax.all_to_all(send_value, ('gx', 'gy'), split_axis=0, con...]
    pallas_call x0 -> x1, Pallas kernels: none -> 29.7 us  [shards(): pl.pallas_call(functools.partial(body, (mx, my, mz, seats, elem_count)),...]
    gather x7 -> x0, local copies, waits for them, and re-layouts: 29.3 us -> none  [the longest x3 17.4 us: shards(): answer = node_disp[:, asked_nodes] * valid.astype(jnp.float32)]
    ppermute x24 -> x0, waiting for transfers between devices: 12.8 us -> none  [the longest x12 8.53 us: padded_2(): lax.ppermute(head, axis, [((i + 1) % count, i) for i in range(ends)])]
    reduce_sum x6 -> x0, other arithmetic: 10.6 us -> none  [the longest x2 7.67 us: ionic(): jnp.sum(conductance.reshape(shape) * gates * (volt[None] - reversal.resha...]
    select_n x12 -> x0, other arithmetic: 7.25 us -> none  [the longest x1 2.11 us: ionic(): calcium = jnp.where(alive, calcium, states[NSTATE - 1])]
  transfers between devices with their start and end apart: 30 -> 0, of which waited for: 8 -> 0; matrix products, arithmetic and copies ran while one was open for 49% -> 0% of each run, Pallas kernels for 0% -> 0%
where the time goes in v1:
time: 40.8 us; the launch traced here: 40.5 us
  Pallas kernels  29.7 us (73%)
  local copies, waits for them, and re-layouts  10.1 us (25%)
  between operations  0.66 us (2%)
    pallas_call x1, Pallas kernels, shards(): pl.pallas_call(functools.partial(body, (mx, my, mz, seats, elem_count)),...  29.7 us
    unnamed x10, local copies, waits for them, and re-layouts  8.81 us

profile of v1, /device:TPU:0, one launch (start us, length us, event | category | flops | bytes accessed | tf_op | source)
XLA Modules:
  0.0 40.5 jit_solution(4046922559883303894)
XLA Ops:
  0.6 1.3 %copy.21.active = s32[2,1,1]{2,1,0:T(1,128)} copy(s32[2,1,1]{0,2,1:T(1,128)} %param.17) | data formatting | bytes 16 | tf_op args[1]
  1.9 1.3 %copy.22.fibre_index = s32[2,1,1]{2,1,0:T(1,128)} copy(s32[2,1,1]{0,2,1:T(1,128)} %param.18) | data formatting | bytes 16 | tf_op args[2]
  3.2 0.7 %copy.19 = s32[4,8,8]{2,1,0:T(8,128)S(1)} copy(s32[4,8,8]{2,0,1:T(4,128)} %bitcast.4) | data formatting | bytes 2048 | tf_op jit(solution)/shard_map/transpose | solution.py:544
  3.9 0.6 %reshape.15.ids_ref = s32[1,256]{1,0:T(1,128)} reshape(s32[4,8,8]{2,1,0:T(8,128)S(1)} %copy.19) | data formatting | bytes 2048 | tf_op jit(solution)/shard_map/reshape | solution.py:544
  4.6 1.4 %copy.20 = f32[8,8,4]{2,1,0:T(8,128)} copy(f32[8,8,4]{1,2,0:T(4,128)} %param.27) | data formatting | bytes 2048 | tf_op args[11]
  6.0 29.7 %step.1 = (f32[19,16,16,128]{3,2,1,0:T(8,128)}, f32[3,16,16,128]{3,2,1,0:T(8,128)}, f32[3,512]{1,0:T(4,128)}) custom-call(f32[19,16,16,128]{3,2,1,0:T(8,128)} %states.1, s32[2,1,1]{2,1,0:T(1,128)} %copy.21.active, s32[2,1,1]{2,1,0:T(1,128)} %copy.22.fibre_index, f32[2,64]{1,0:T(2,128)} %angle_v.1, f32[2,64]{1,0:T(2,128)} %angle_v.1, f32[2,64]{1,0:T(2,128)} %conduct.1, ...), custom_call_target="tpu_custom_call" | custom-call | tf_op jit(solution)/shard_map/step/pallas_call | solution.py:549
  35.7 0.0 copy-start
  35.7 0.0 copy-start.1
  35.7 3.4 %copy.26 = f32[19,16,16,128]{3,2,1,0:T(8,128)} copy(f32[19,16,16,128]{3,2,1,0:T(8,128)} %get-tuple-element.6) | data formatting | bytes 4980736
  39.1 0.0 copy-done
  39.2 0.7 %copy.27 = f32[3,16,16,128]{3,2,1,0:T(8,128)} copy(f32[3,16,16,128]{3,2,1,0:T(8,128)S(1)} %copy-done) | data formatting | bytes 786432
  39.9 0.0 copy-done.1
  39.9 0.6 %copy.28 = f32[3,512]{1,0:T(4,128)} copy(f32[3,512]{1,0:T(4,128)S(1)} %copy-done.1) | data formatting | bytes 12288
Async XLA Ops:
  35.7 3.4 %copy-start = (f32[3,16,16,128]{3,2,1,0:T(8,128)S(1)}, f32[3,16,16,128]{3,2,1,0:T(8,128)}, u32[]{:S(2)}) copy-start(f32[3,16,16,128]{3,2,1,0:T(8,128)} %get-tuple-element.7) | copy-start | bytes 1179652
  35.7 4.2 %copy-start.1 = (f32[3,512]{1,0:T(4,128)S(1)}, f32[3,512]{1,0:T(4,128)}, u32[]{:S(2)}) copy-start(f32[3,512]{1,0:T(4,128)} %get-tuple-element.8) | copy-start | bytes 18436

commit v2 on v1

--- a/solution.py
+++ b/solution.py
@@ -160,11 +160,11 @@
 
     coef, live = [], []
     for t in range(tiles):
-        index = fibre_index[t, 0, 0]
+        index = fibre_index[0, 0, t]
         fx, fy, fz = frame_of(splat(angle_s[0, index]), splat(angle_s[1, index]))
         across = splat(conduct[1, index])
         spread = splat(conduct[0, index]) - across
-        alive = splat(jnp.where(active[t, 0, 0] > 0, 1.0, 0.0).astype(f32))
+        alive = splat(jnp.where(active[0, 0, t] > 0, 1.0, 0.0).astype(f32))
         live.append(alive)
         coef.append(
             [
@@ -341,7 +341,19 @@
     for t in range(tiles):
         ionic(states, t)
     shift = elem_count.bit_length() - 1
-    ids = ids_ref[...]
+
+    def flat_row(ref):
+        place = lax.rem(iota((by, blocks), 1), plane)
+        spread = jnp.zeros((bz, blocks), f32)
+        for i in range(bx):
+            put = onehot(place == iota((by, blocks), 0) + i * by)
+            for part in parts3(ref[i].astype(f32)):
+                spread = spread + mm(part, put)
+        mine = iota((bz, blocks), 1) // plane == iota((bz, blocks), 0)
+        return jnp.sum(jnp.where(mine, spread, 0.0), axis=0, keepdims=True)
+
+    ids = flat_row(ids_ref).astype(jnp.int32)
+    weight_col = column(flat_row(weight_ref))
     owner = lax.shift_right_logical(ids, shift)
     local = ids - owner * elem_count
     owner_col = column(owner.astype(f32))
@@ -405,12 +417,12 @@
     pooled = fold3(mm(rows3(pooled), strip)) * (1.0 / (SBX * SBY * SBZ))
     worth = jnp.concatenate(
         [
-            jnp.broadcast_to(pooled[:, b : b + 1] * weight_ref[:, b : b + 1], (plane, LANES))
+            jnp.broadcast_to(pooled[:, b : b + 1], (plane, LANES))
             for b in range(bz)
         ],
         0,
     )
-    worth = jnp.where(rank_oh[...].astype(f32) > 0.5, worth, 0.0)
+    worth = jnp.where(rank_oh[...].astype(f32) > 0.5, worth * weight_col, 0.0)
     val_send[...] = mm_right3(owner_oh[...], worth).reshape(n, 1, LANES)
     all_start(2, val_send, val_got)
 
@@ -541,8 +553,8 @@
     blocks = bx * by * bz
     seats = max(2 * blocks // n, 8)
     slots = n * seats
-    ids = block_elem.transpose(2, 0, 1).reshape(1, blocks)
-    weight = block_weight.reshape(bx * by, bz)
+    ids = block_elem.transpose(0, 2, 1)
+    weight = block_weight.transpose(0, 2, 1)
     vmem = pl.BlockSpec(memory_space=pltpu.VMEM)
     smem = pl.BlockSpec(memory_space=pltpu.SMEM)
     stages = 2 * FINE_STEPS
@@ -586,8 +598,8 @@
         name="step",
     )(
         states,
-        active,
-        fibre_index,
+        active.transpose(1, 2, 0),
+        fibre_index.transpose(1, 2, 0),
         fibre_angle,
         fibre_angle,
         conduct,

time: 40.8 us -> 35.5 us (0.87)
  local copies, waits for them, and re-layouts: 10.1 us -> 4.77 us
    unnamed x10 -> x7, local copies, waits for them, and re-layouts: 8.81 us -> 4.77 us
    transpose x1 -> x0, local copies, waits for them, and re-layouts: 0.72 us -> none  [shards(): ids = block_elem.transpose(2, 0, 1).reshape(1, blocks)]
    reshape x1 -> x0, local copies, waits for them, and re-layouts: 0.62 us -> none  [shards(): ids = block_elem.transpose(2, 0, 1).reshape(1, blocks)]
where the time goes in v2:
time: 35.5 us; the launch traced here: 35.3 us
  Pallas kernels  29.9 us (84%)
  local copies, waits for them, and re-layouts  4.77 us (13%)
  between operations  0.66 us (2%)
    pallas_call x1, Pallas kernels, shards(): pl.pallas_call(functools.partial(body, (mx, my, mz, seats, elem_count)),...  29.9 us
    unnamed x7, local copies, waits for them, and re-layouts  4.77 us

profile of v2, /device:TPU:0, one launch (start us, length us, event | category | flops | bytes accessed | tf_op | source)
XLA Modules:
  0.0 35.3 jit_solution(339581504646815656)
XLA Ops:
  0.6 29.9 %step.1 = (f32[19,16,16,128]{3,2,1,0:T(8,128)}, f32[3,16,16,128]{3,2,1,0:T(8,128)}, f32[3,512]{1,0:T(4,128)}) custom-call(f32[19,16,16,128]{3,2,1,0:T(8,128)} %states.1, s32[1,1,2]{2,1,0:T(1,128)} %bitcast.8, s32[1,1,2]{2,1,0:T(1,128)} %bitcast.9, f32[2,64]{1,0:T(2,128)} %angle_v.1, f32[2,64]{1,0:T(2,128)} %angle_v.1, f32[2,64]{1,0:T(2,128)} %conduct.1, ...), custom_call_target="tpu_custom_call" | custom-call | tf_op jit(solution)/shard_map/step/pallas_call | solution.py:561
  30.5 0.0 copy-start
  30.5 0.0 copy-start.1
  30.6 3.4 %copy.22 = f32[19,16,16,128]{3,2,1,0:T(8,128)} copy(f32[19,16,16,128]{3,2,1,0:T(8,128)} %get-tuple-element.6) | data formatting | bytes 4980736
  34.0 0.0 copy-done
  34.0 0.7 %copy.23 = f32[3,16,16,128]{3,2,1,0:T(8,128)} copy(f32[3,16,16,128]{3,2,1,0:T(8,128)S(1)} %copy-done) | data formatting | bytes 786432
  34.7 0.0 copy-done.1
  34.7 0.6 %copy.24 = f32[3,512]{1,0:T(4,128)} copy(f32[3,512]{1,0:T(4,128)S(1)} %copy-done.1) | data formatting | bytes 12288
Async XLA Ops:
  30.5 3.4 %copy-start = (f32[3,16,16,128]{3,2,1,0:T(8,128)S(1)}, f32[3,16,16,128]{3,2,1,0:T(8,128)}, u32[]{:S(2)}) copy-start(f32[3,16,16,128]{3,2,1,0:T(8,128)} %get-tuple-element.7) | copy-start | bytes 1179652
  30.5 4.2 %copy-start.1 = (f32[3,512]{1,0:T(4,128)S(1)}, f32[3,512]{1,0:T(4,128)}, u32[]{:S(2)}) copy-start(f32[3,512]{1,0:T(4,128)} %get-tuple-element.8) | copy-start | bytes 18436
